TPU v7x, 32 devices: a whole 2x2x4 slice. The times are simulated.
32 devices in a mesh: outer: 4 (over y, core), inner: 8 (over z, x).
Axes of the slice: x: 2, y: 2, z: 4, core: 2. Of those that a mesh axis runs over, the one named last changes fastest.
Arguments:
- queries: bfloat16 [4096, 2048], P(('outer', 'inner')), may hold values from -6 to 6
- keys: bfloat16 [4096, 2048], P(('outer', 'inner')), may hold values from -6 to 6
- values: bfloat16 [4096, 2048], P(('outer', 'inner')), may hold values from -6 to 6
- gain: float32 [2048], replicated, may hold values from 0.5 to 1.5
Outputs:
- attended: bfloat16 [4096, 2048], P(('outer', 'inner'))
All inputs are finite; a program needn't handle non-finite values.
Results may differ from a plain program's by a relative error of at most 0.0049.
Values sent between devices are 32-bit elements; how exact they have to be, the bound alone decides.
No kernel may reach another device: no remote copies, remote signals or barrier semaphores. Data moves between devices by JAX's collectives and lax.ppermute only.
A program may use at most 64 MiB of HBM per device.

v0:
```python
import functools

import jax
import jax.numpy as jnp
from jax import lax
from jax.experimental import pallas as pl
from jax.experimental.pallas import tpu as pltpu
from jax.sharding import PartitionSpec as P

D = 128
WAYS = 4
COUNTS = (8, 8)
AXES = ("outer", "inner")
F32 = jnp.float32
BF16 = jnp.bfloat16
SMALL = pltpu.CompilerParams(vmem_limit_bytes=8 << 20)


def cost(flops, moved):
    return pl.CostEstimate(flops=flops, bytes_accessed=moved, transcendentals=0)


def emit_states(place_rows, heads, base, low, k_ref, v_ref, whole_ref, out_refs):
    for j in range(heads):
        at = pl.ds(base + j * D, D)
        whole_ref[j] = lax.dot_general(
            k_ref[:, at], v_ref[:, at], (((0,), (0,)), ((), ())), preferred_element_type=F32
        )
        for place, out_ref in enumerate(out_refs):
            start = pl.multiple_of((low ^ place) * place_rows, place_rows)
            out_ref[j] = whole_ref[j, pl.ds(start, place_rows), :]


def first_body(heads, low_ref, k_hbm, v_hbm, *refs):
    out_refs, (k_buf, v_buf, whole_ref, sems) = refs[:WAYS], refs[WAYS:]
    at = pl.ds(0, heads * D)
    copies = [
        pltpu.make_async_copy(k_hbm.at[:, at], k_buf, sems.at[0]),
        pltpu.make_async_copy(v_hbm.at[:, at], v_buf, sems.at[1]),
    ]
    for copy in copies:
        copy.start()
    for copy in copies:
        copy.wait()
    emit_states(D // WAYS, heads, 0, low_ref[0], k_buf, v_buf, whole_ref, out_refs)


def first_states(low, keys, values, heads):
    rows = keys.shape[0]
    shape = (heads, D // WAYS, D)
    return pl.pallas_call(
        functools.partial(first_body, heads),
        grid_spec=pltpu.PrefetchScalarGridSpec(
            num_scalar_prefetch=1,
            grid=(1,),
            in_specs=[pl.BlockSpec(memory_space=pltpu.HBM)] * 2,
            out_specs=[pl.BlockSpec(shape, lambda i, low: (0, 0, 0))] * WAYS,
            scratch_shapes=[
                pltpu.VMEM((rows, heads * D), BF16),
                pltpu.VMEM((rows, heads * D), BF16),
                pltpu.VMEM((heads, D, D), F32),
                pltpu.SemaphoreType.DMA((2,)),
            ],
        ),
        out_shape=[jax.ShapeDtypeStruct(shape, F32)] * WAYS,
        cost_estimate=cost(2 * rows * D * D * heads, rows * D * heads * 4 + heads * D * D * 4),
        compiler_params=SMALL,
        name="first_states",
    )(low, keys, values)


def states_body(counts, skip, low_ref, k_ref, v_ref, *refs):
    out_refs, whole_ref = refs[:-1], refs[-1]
    base = skip
    for i, heads in enumerate(counts):
        emit_states(
            D // WAYS, heads, base * D, low_ref[0], k_ref, v_ref, whole_ref, out_refs[i * WAYS : (i + 1) * WAYS]
        )
        base += heads


def block_states(low, keys, values, counts, skip):
    rows, width = keys.shape
    heads = sum(counts)
    shapes = [(n, D // WAYS, D) for n in counts for _ in range(WAYS)]
    spec = pl.BlockSpec((rows, width), lambda i, low: (0, 0))
    return pl.pallas_call(
        functools.partial(states_body, counts, skip),
        grid_spec=pltpu.PrefetchScalarGridSpec(
            num_scalar_prefetch=1,
            grid=(1,),
            in_specs=[spec, spec],
            out_specs=[pl.BlockSpec(shape, lambda i, low: (0, 0, 0)) for shape in shapes],
            scratch_shapes=[pltpu.VMEM((max(counts), D, D), F32)],
        ),
        out_shape=[jax.ShapeDtypeStruct(shape, F32) for shape in shapes],
        cost_estimate=cost(2 * rows * D * D * heads, rows * D * heads * 4 + heads * D * D * 4),
        compiler_params=SMALL,
        name="block_states",
    )(low, keys, values)


def within_body(heads, low_ref, q_ref, k_ref, v_ref, out_ref, turned_ref):
    rows = q_ref.shape[0]
    row = lax.broadcasted_iota(jnp.int32, (rows, rows), 0)
    keep = row >= lax.broadcasted_iota(jnp.int32, (rows, rows), 1)
    lane = lax.broadcasted_iota(jnp.int32, (D, D), 1)
    place_rows = D // WAYS
    source = ((lane // place_rows) ^ low_ref[0]) * place_rows + lane % place_rows
    turn = jnp.where(lax.broadcasted_iota(jnp.int32, (D, D), 0) == source, 1.0, 0.0).astype(BF16)
    for h in range(heads):
        at = pl.ds(h * D, D)
        scores = lax.dot_general(
            q_ref[:, at], k_ref[:, at], (((1,), (1,)), ((), ())), preferred_element_type=F32
        )
        scores = jnp.where(keep, scores, 0.0).astype(BF16)
        out_ref[:, at] = jnp.dot(scores, v_ref[:, at], preferred_element_type=F32)
        turned_ref[:, at] = jnp.dot(q_ref[:, at], turn, preferred_element_type=F32).astype(BF16)


def within_block(low, queries, keys, values):
    rows, width = queries.shape
    spec = pl.BlockSpec((rows, width), lambda i, low: (0, 0))
    return pl.pallas_call(
        functools.partial(within_body, width // D),
        grid_spec=pltpu.PrefetchScalarGridSpec(
            num_scalar_prefetch=1, grid=(1,), in_specs=[spec] * 3, out_specs=[spec] * 2
        ),
        out_shape=[jax.ShapeDtypeStruct((rows, width), F32), jax.ShapeDtypeStruct((rows, width), BF16)],
        cost_estimate=cost(6 * rows * rows * width, rows * width * 12),
        compiler_params=SMALL,
        name="within_block",
    )(low, queries, keys, values)


def finish_body(heads, base, q_ref, near_ref, gain_ref, *refs):
    state_refs, (out_hbm, block, sem) = refs[:WAYS], refs[-3:]
    for j in range(heads):
        state = jnp.concatenate([ref[j] for ref in state_refs], axis=0).astype(BF16)
        at = pl.ds((base + j) * D, D)
        raw = near_ref[:, at] + jnp.dot(q_ref[:, at], state, preferred_element_type=F32)
        scale = lax.rsqrt(jnp.mean(raw * raw, axis=-1, keepdims=True) + 1e-06)
        block[:, pl.ds(j * D, D)] = (raw * scale * gain_ref[:, at]).astype(BF16)
    copy = pltpu.make_async_copy(block, out_hbm.at[:, pl.ds(base * D, heads * D)], sem)
    copy.start()
    copy.wait()


def finish(turned, near, gain, states, heads, base, out):
    rows, width = turned.shape
    spec = pl.BlockSpec(memory_space=pltpu.VMEM)
    extra = [] if out is None else [out]
    return pl.pallas_call(
        functools.partial(finish_body, heads, base),
        in_specs=[spec] * 3
        + [spec] * WAYS
        + [pl.BlockSpec(memory_space=pltpu.HBM)] * len(extra),
        out_specs=pl.BlockSpec(memory_space=pltpu.HBM),
        scratch_shapes=[pltpu.VMEM((rows, heads * D), BF16), pltpu.SemaphoreType.DMA],
        out_shape=jax.ShapeDtypeStruct((rows, width), BF16),
        input_output_aliases={} if out is None else {3 + WAYS: 0},
        cost_estimate=cost(2 * rows * D * D * heads, rows * D * heads * 8 + heads * D * D * 4),
        compiler_params=SMALL,
        name="finish",
    )(turned, near, gain, *states, *extra)


ORDER = (1, 3, 2)


def on_device(size, queries, keys, values, gain):
    _, width = queries.shape
    rank = lax.axis_index(AXES)
    low = rank % WAYS
    low_arr = jnp.full((1,), low, jnp.int32)
    gain = gain.reshape(1, width)
    bits = [1 << b for b in range(2, size.bit_length() - 1)]

    def flip(value, mask):
        return lax.ppermute(value, AXES, [(d, d ^ mask) for d in range(size)])

    finals = []
    first = first_states(
        low_arr,
        pltpu.with_memory_space_constraint(keys, pltpu.HBM),
        pltpu.with_memory_space_constraint(values, pltpu.HBM),
        COUNTS[0],
    )
    rest = block_states(low_arr, keys, values, COUNTS[1:], COUNTS[0])
    states = list(first) + list(rest)
    near, turned = within_block(low_arr, queries, keys, values)
    for c in range(len(COUNTS)):
        own = states[c * WAYS : (c + 1) * WAYS]
        pieces = {0: own[0]}
        for r in ORDER:
            pieces[r] = flip(own[r], r)
        total = functools.reduce(jnp.add, [pieces[r] for r in range(WAYS)])
        before = jnp.zeros_like(total)
        for b in bits:
            other = flip(total, b)
            before = before + jnp.where(rank & b != 0, other, 0.0)
            total = total + other
        carried = []
        for s in range(WAYS):
            part = before
            for r in range(WAYS):
                if r != s:
                    part = part + jnp.where((low ^ r) < (low ^ s), pieces[r], 0.0)
            carried.append(part)
        got = {0: carried[0]}
        for s in ORDER:
            got[s] = flip(carried[s], s)
        finals.append([got[s] for s in range(WAYS)])
    out = None
    for c, heads in enumerate(COUNTS):
        out = finish(turned, near, gain, finals[c], heads, sum(COUNTS[:c]), out)
    return out


def solution(mesh):
    size = mesh.shape["outer"] * mesh.shape["inner"]

    def body(*args):
        return on_device(size, *args)

    return jax.shard_map(
        body,
        mesh=mesh,
        in_specs=(P(AXES, None), P(AXES, None), P(AXES, None), P()),
        out_specs=P(AXES, None),
        check_vma=False,
    )
```

profile of v0, /device:TPU:0, one launch (start us, length us, event | category | flops | bytes accessed | tf_op | source)
XLA Modules:
  0.0 49.7 jit_solution(12579672742083672924)
XLA Ops:
  0.0 1.4 %first_states.1 = (f32[8,32,128]{2,1,0:T(8,128)S(1)}, f32[8,32,128]{2,1,0:T(8,128)S(1)}, f32[8,32,128]{2,1,0:T(8,128)S(1)}, f32[8,32,128]{2,1,0:T(8,128)S(1)}) custom-call(s32[1]{0:T(128)} %bitcast.low_ref, bf16[128,2048]{1,0:T(8,128)(2,1)} %k_hbm.1, bf16[128,2048]{1,0:T(8,128)(2,1)} %v_hbm.1), custom_call_target="tpu_custom_call" | custom-call | flops 33554432 | bytes 1048576 | tf_op jit(solution)/shard_map/first_states/pallas_call | solution.py:51
  1.4 3.0 %collective-permute-start.9 = (f32[8,32,128]{2,1,0:T(8,128)S(1)}, f32[8,32,128]{2,1,0:T(8,128)S(1)}, u32[]{:S(2)}, u32[]{:S(2)}) collective-permute-start(f32[8,32,128]{2,1,0:T(8,128)S(1)} %get-tuple-element.22), channel_id=1, source_target_pairs={{0,1},{1,0},{2,3},{3,2},{4,5},{5,4},{6,7},{7,6},{8,9},{9,8},{10,11... | collective-permute-start | bytes 393224 | tf_op jit(solution)/shard_map/ppermute | solution.py:180
  4.5 1.6 %collective-permute-start.10 = (f32[8,32,128]{2,1,0:T(8,128)S(1)}, f32[8,32,128]{2,1,0:T(8,128)S(1)}, u32[]{:S(2)}, u32[]{:S(2)}) collective-permute-start(f32[8,32,128]{2,1,0:T(8,128)S(1)} %get-tuple-element.23), channel_id=1, source_target_pairs={{0,2},{1,3},{2,0},{3,1},{4,6},{5,7},{6,4},{7,5},{8,10},{9,11},{10,... | collective-permute-start | bytes 393224 | tf_op jit(solution)/shard_map/ppermute | solution.py:180
  6.1 0.3 block_states.1
  6.4 2.0 %collective-permute-start = (f32[8,32,128]{2,1,0:T(8,128)S(1)}, f32[8,32,128]{2,1,0:T(8,128)S(1)}, u32[]{:S(2)}, u32[]{:S(2)}) collective-permute-start(f32[8,32,128]{2,1,0:T(8,128)S(1)} %get-tuple-element.18), channel_id=1, source_target_pairs={{0,1},{1,0},{2,3},{3,2},{4,5},{5,4},{6,7},{7,6},{8,9},{9,8},{10,11... | collective-permute-start | bytes 393224 | tf_op jit(solution)/shard_map/ppermute | solution.py:180
  8.3 1.6 %collective-permute-start.1 = (f32[8,32,128]{2,1,0:T(8,128)S(1)}, f32[8,32,128]{2,1,0:T(8,128)S(1)}, u32[]{:S(2)}, u32[]{:S(2)}) collective-permute-start(f32[8,32,128]{2,1,0:T(8,128)S(1)} %get-tuple-element.19), channel_id=1, source_target_pairs={{0,2},{1,3},{2,0},{3,1},{4,6},{5,7},{6,4},{7,5},{8,10},{9,11},{10,... | collective-permute-start | bytes 393224 | tf_op jit(solution)/shard_map/ppermute | solution.py:180
  9.9 1.0 %collective-permute-start.2 = (f32[8,32,128]{2,1,0:T(8,128)S(1)}, f32[8,32,128]{2,1,0:T(8,128)S(1)}, u32[]{:S(2)}, u32[]{:S(2)}) collective-permute-start(f32[8,32,128]{2,1,0:T(8,128)S(1)} %get-tuple-element.20), channel_id=1, source_target_pairs={{0,3},{1,2},{2,1},{3,0},{4,7},{5,6},{6,5},{7,4},{8,11},{9,10},{10,... | collective-permute-start | bytes 393224 | tf_op jit(solution)/shard_map/ppermute | solution.py:180
  11.0 2.4 %collective-permute-done.11 = f32[8,32,128]{2,1,0:T(8,128)S(1)} collective-permute-done((f32[8,32,128]{2,1,0:T(8,128)S(1)}, f32[8,32,128]{2,1,0:T(8,128)S(1)}, u32[]{:S(2)}, u32[]{:S(2)}) %collective-permute-start.11) | collective-permute-done | bytes 131104 | tf_op jit(solution)/shard_map/ppermute | solution.py:180
  13.4 2.7 %collective-permute-start.12 = (f32[8,32,128]{2,1,0:T(8,128)S(1)}, f32[8,32,128]{2,1,0:T(8,128)S(1)}, u32[]{:S(2)}, u32[]{:S(2)}) collective-permute-start(f32[8,32,128]{2,1,0:T(8,128)S(1)} %add_add_fusion), channel_id=1, source_target_pairs={{0,4},{1,5},{2,6},{3,7},{4,0},{5,1},{6,2},{7,3},{8,12},{9,13},{10,... | collective-permute-start | bytes 393224 | tf_op jit(solution)/shard_map/ppermute | solution.py:180
  16.1 1.8 %collective-permute-done.1 = f32[8,32,128]{2,1,0:T(8,128)S(1)} collective-permute-done((f32[8,32,128]{2,1,0:T(8,128)S(1)}, f32[8,32,128]{2,1,0:T(8,128)S(1)}, u32[]{:S(2)}, u32[]{:S(2)}) %collective-permute-start.1) | collective-permute-done | bytes 131104 | tf_op jit(solution)/shard_map/ppermute | solution.py:180
  17.9 1.3 %collective-permute-done.2 = f32[8,32,128]{2,1,0:T(8,128)S(1)} collective-permute-done((f32[8,32,128]{2,1,0:T(8,128)S(1)}, f32[8,32,128]{2,1,0:T(8,128)S(1)}, u32[]{:S(2)}, u32[]{:S(2)}) %collective-permute-start.2) | collective-permute-done | bytes 131104 | tf_op jit(solution)/shard_map/ppermute | solution.py:180
  19.2 2.5 %collective-permute-start.3 = (f32[8,32,128]{2,1,0:T(8,128)S(1)}, f32[8,32,128]{2,1,0:T(8,128)S(1)}, u32[]{:S(2)}, u32[]{:S(2)}) collective-permute-start(f32[8,32,128]{2,1,0:T(8,128)S(1)} %add_add_fusion.1), channel_id=1, source_target_pairs={{0,4},{1,5},{2,6},{3,7},{4,0},{5,1},{6,2},{7,3},{8,12},{9,13},{10,... | collective-permute-start | bytes 393224 | tf_op jit(solution)/shard_map/ppermute | solution.py:180
  21.8 6.5 %collective-permute-done.3 = f32[8,32,128]{2,1,0:T(8,128)S(1)} collective-permute-done((f32[8,32,128]{2,1,0:T(8,128)S(1)}, f32[8,32,128]{2,1,0:T(8,128)S(1)}, u32[]{:S(2)}, u32[]{:S(2)}) %collective-permute-start.3) | collective-permute-done | bytes 131104 | tf_op jit(solution)/shard_map/ppermute | solution.py:180
  28.3 0.1 collective-permute-start.4
  28.5 1.6 %collective-permute-start.14 = (f32[8,32,128]{2,1,0:T(8,128)S(1)}, f32[8,32,128]{2,1,0:T(8,128)S(1)}, u32[]{:S(2)}, u32[]{:S(2)}) collective-permute-start(f32[8,32,128]{2,1,0:T(8,128)S(1)} %add.147), channel_id=1, source_target_pairs={{0,16},{1,17},{2,18},{3,19},{4,20},{5,21},{6,22},{7,23},{8,24},{9,... | collective-permute-start | bytes 393224 | tf_op jit(solution)/shard_map/ppermute | solution.py:180
  30.1 1.3 %collective-permute-start.5 = (f32[8,32,128]{2,1,0:T(8,128)S(1)}, f32[8,32,128]{2,1,0:T(8,128)S(1)}, u32[]{:S(2)}, u32[]{:S(2)}) collective-permute-start(f32[8,32,128]{2,1,0:T(8,128)S(1)} %add.128), channel_id=1, source_target_pairs={{0,16},{1,17},{2,18},{3,19},{4,20},{5,21},{6,22},{7,23},{8,24},{9,... | collective-permute-start | bytes 393224 | tf_op jit(solution)/shard_map/ppermute | solution.py:180
  31.4 3.5 %collective-permute-done.14 = f32[8,32,128]{2,1,0:T(8,128)S(1)} collective-permute-done((f32[8,32,128]{2,1,0:T(8,128)S(1)}, f32[8,32,128]{2,1,0:T(8,128)S(1)}, u32[]{:S(2)}, u32[]{:S(2)}) %collective-permute-start.14) | collective-permute-done | bytes 131104 | tf_op jit(solution)/shard_map/ppermute | solution.py:180
  35.0 0.1 select_add_fusion.1
  35.1 1.1 %collective-permute-start.15 = (f32[8,32,128]{2,1,0:T(8,128)S(1)}, f32[8,32,128]{2,1,0:T(8,128)S(1)}, u32[]{:S(2)}, u32[]{:S(2)}) collective-permute-start(f32[8,32,128]{2,1,0:T(8,128)S(1)} %get-tuple-element.30), channel_id=1, source_target_pairs={{0,1},{1,0},{2,3},{3,2},{4,5},{5,4},{6,7},{7,6},{8,9},{9,8},{10,11... | collective-permute-start | bytes 393224 | tf_op jit(solution)/shard_map/ppermute | solution.py:180
  36.2 2.4 %collective-permute-start.17 = (f32[8,32,128]{2,1,0:T(8,128)S(1)}, f32[8,32,128]{2,1,0:T(8,128)S(1)}, u32[]{:S(2)}, u32[]{:S(2)}) collective-permute-start(f32[8,32,128]{2,1,0:T(8,128)S(1)} %get-tuple-element.25), channel_id=1, source_target_pairs={{0,3},{1,2},{2,1},{3,0},{4,7},{5,6},{6,5},{7,4},{8,11},{9,10},{10,... | collective-permute-start | bytes 393224 | tf_op jit(solution)/shard_map/ppermute | solution.py:180
  38.7 0.1 select_add_fusion.6
  38.8 0.1 collective-permute-start.7
  38.9 1.0 %collective-permute-start.6 = (f32[8,32,128]{2,1,0:T(8,128)S(1)}, f32[8,32,128]{2,1,0:T(8,128)S(1)}, u32[]{:S(2)}, u32[]{:S(2)}) collective-permute-start(f32[8,32,128]{2,1,0:T(8,128)S(1)} %get-tuple-element.33), channel_id=1, source_target_pairs={{0,1},{1,0},{2,3},{3,2},{4,5},{5,4},{6,7},{7,6},{8,9},{9,8},{10,11... | collective-permute-start | bytes 393224 | tf_op jit(solution)/shard_map/ppermute | solution.py:180
  40.0 1.5 %collective-permute-done.16.refs_2_ = f32[8,32,128]{2,1,0:T(8,128)S(1)} collective-permute-done((f32[8,32,128]{2,1,0:T(8,128)S(1)}, f32[8,32,128]{2,1,0:T(8,128)S(1)}, u32[]{:S(2)}, u32[]{:S(2)}) %collective-permute-start.16) | collective-permute-done | bytes 131104 | tf_op jit(solution)/shard_map/ppermute | solution.py:180
  41.5 0.9 %collective-permute-start.8 = (f32[8,32,128]{2,1,0:T(8,128)S(1)}, f32[8,32,128]{2,1,0:T(8,128)S(1)}, u32[]{:S(2)}, u32[]{:S(2)}) collective-permute-start(f32[8,32,128]{2,1,0:T(8,128)S(1)} %get-tuple-element.27), channel_id=1, source_target_pairs={{0,3},{1,2},{2,1},{3,0},{4,7},{5,6},{6,5},{7,4},{8,11},{9,10},{10,... | collective-permute-start | bytes 393224 | tf_op jit(solution)/shard_map/ppermute | solution.py:180
  42.4 0.9 %within_block.1 = (f32[128,2048]{1,0:T(8,128)S(1)}, bf16[128,2048]{1,0:T(8,128)(2,1)S(1)}) custom-call(s32[1]{0:T(128)} %bitcast.low_ref, bf16[128,2048]{1,0:T(8,128)(2,1)S(1)} %copy-done.2, bf16[128,2048]{1,0:T(8,128)(2,1)S(1)} %copy-done, bf16[128,2048]{1,0:T(8,128)(2,1)S(1)} %copy-done.1), custom_call_target="tpu_custom_call" | custom-call | flops 201326592 | bytes 3145728 | tf_op jit(solution)/shard_map/within_block/pallas_call | solution.py:124
  43.3 1.6 %collective-permute-done.17.refs_3_ = f32[8,32,128]{2,1,0:T(8,128)S(1)} collective-permute-done((f32[8,32,128]{2,1,0:T(8,128)S(1)}, f32[8,32,128]{2,1,0:T(8,128)S(1)}, u32[]{:S(2)}, u32[]{:S(2)}) %collective-permute-start.17) | collective-permute-done | bytes 131104 | tf_op jit(solution)/shard_map/ppermute | solution.py:180
  44.9 1.1 %finish.2.refs_4_ = bf16[128,2048]{1,0:T(8,128)(2,1)} custom-call(bf16[128,2048]{1,0:T(8,128)(2,1)S(1)} %get-tuple-element.15.q_ref, f32[128,2048]{1,0:T(8,128)S(1)} %get-tuple-element.16.near_ref, f32[1,2048]{1,0:T(1,128)S(1)} %bitcast.2, f32[8,32,128]{2,1,0:T(8,128)S(1)} %get-tuple-element.31.refs_0_, f32[8,32,128]{2,1,0:T(8,128)S(1)} %collective-permute-done.15.refs_1_, ...), custom_call_target="tpu_custom_call" | custom-call | flops 33554432 | bytes 1572864 | tf_op jit(solution)/shard_map/finish/pallas_call | solution.py:153
  46.0 0.7 %collective-permute-done.7.refs_2_ = f32[8,32,128]{2,1,0:T(8,128)S(1)} collective-permute-done((f32[8,32,128]{2,1,0:T(8,128)S(1)}, f32[8,32,128]{2,1,0:T(8,128)S(1)}, u32[]{:S(2)}, u32[]{:S(2)}) %collective-permute-start.7) | collective-permute-done | bytes 131104 | tf_op jit(solution)/shard_map/ppermute | solution.py:180
  46.7 0.5 collective-permute-done.6.refs_1_
  47.2 1.4 %collective-permute-done.8.refs_3_ = f32[8,32,128]{2,1,0:T(8,128)S(1)} collective-permute-done((f32[8,32,128]{2,1,0:T(8,128)S(1)}, f32[8,32,128]{2,1,0:T(8,128)S(1)}, u32[]{:S(2)}, u32[]{:S(2)}) %collective-permute-start.8) | collective-permute-done | bytes 131104 | tf_op jit(solution)/shard_map/ppermute | solution.py:180
  48.6 1.1 %finish.3 = bf16[128,2048]{1,0:T(8,128)(2,1)} custom-call(bf16[128,2048]{1,0:T(8,128)(2,1)S(1)} %get-tuple-element.15.q_ref, f32[128,2048]{1,0:T(8,128)S(1)} %get-tuple-element.16.near_ref, f32[1,2048]{1,0:T(1,128)S(1)} %bitcast.3, f32[8,32,128]{2,1,0:T(8,128)S(1)} %get-tuple-element.34.refs_0_, ...), custom_call_target="tpu_custom_call", output_to_operand_aliasing={{}: (7, {})} | custom-call | flops 33554432 | bytes 1572864 | tf_op jit(solution)/shard_map/finish/pallas_call | solution.py:153
  (27 shorter events, 0.5 us)
Async XLA Ops:
  0.0 6.1 %copy-start = (bf16[128,2048]{1,0:T(8,128)(2,1)S(1)}, bf16[128,2048]{1,0:T(8,128)(2,1)}, u32[]{:S(2)}) copy-start(bf16[128,2048]{1,0:T(8,128)(2,1)} %k_hbm.1) | copy-start | bytes 1572868
  0.0 6.1 %copy-start.1 = (bf16[128,2048]{1,0:T(8,128)(2,1)S(1)}, bf16[128,2048]{1,0:T(8,128)(2,1)}, u32[]{:S(2)}) copy-start(bf16[128,2048]{1,0:T(8,128)(2,1)} %v_hbm.1) | copy-start | bytes 1572868
  1.4 8.5 %collective-permute-start.9 = (f32[8,32,128]{2,1,0:T(8,128)S(1)}, f32[8,32,128]{2,1,0:T(8,128)S(1)}, u32[]{:S(2)}, u32[]{:S(2)}) collective-permute-start(f32[8,32,128]{2,1,0:T(8,128)S(1)} %get-tuple-element.22), channel_id=1, source_target_pairs={{0,1},{1,0},{2,3},{3,2},{4,5},{5,4},{6,7},{7,6},{8,9},{9,8},{10,11... | collective-permute-start | bytes 393224 | tf_op jit(solution)/shard_map/ppermute | solution.py:180
  4.5 6.5 %collective-permute-start.10 = (f32[8,32,128]{2,1,0:T(8,128)S(1)}, f32[8,32,128]{2,1,0:T(8,128)S(1)}, u32[]{:S(2)}, u32[]{:S(2)}) collective-permute-start(f32[8,32,128]{2,1,0:T(8,128)S(1)} %get-tuple-element.23), channel_id=1, source_target_pairs={{0,2},{1,3},{2,0},{3,1},{4,6},{5,7},{6,4},{7,5},{8,10},{9,11},{10,... | collective-permute-start | bytes 393224 | tf_op jit(solution)/shard_map/ppermute | solution.py:180
  6.1 7.3 %collective-permute-start.11 = (f32[8,32,128]{2,1,0:T(8,128)S(1)}, f32[8,32,128]{2,1,0:T(8,128)S(1)}, u32[]{:S(2)}, u32[]{:S(2)}) collective-permute-start(f32[8,32,128]{2,1,0:T(8,128)S(1)} %get-tuple-element.24), channel_id=1, source_target_pairs={{0,3},{1,2},{2,1},{3,0},{4,7},{5,6},{6,5},{7,4},{8,11},{9,10},{10,... | collective-permute-start | bytes 393224 | tf_op jit(solution)/shard_map/ppermute | solution.py:180
  6.4 9.7 %collective-permute-start = (f32[8,32,128]{2,1,0:T(8,128)S(1)}, f32[8,32,128]{2,1,0:T(8,128)S(1)}, u32[]{:S(2)}, u32[]{:S(2)}) collective-permute-start(f32[8,32,128]{2,1,0:T(8,128)S(1)} %get-tuple-element.18), channel_id=1, source_target_pairs={{0,1},{1,0},{2,3},{3,2},{4,5},{5,4},{6,7},{7,6},{8,9},{9,8},{10,11... | collective-permute-start | bytes 393224 | tf_op jit(solution)/shard_map/ppermute | solution.py:180
  8.3 9.5 %collective-permute-start.1 = (f32[8,32,128]{2,1,0:T(8,128)S(1)}, f32[8,32,128]{2,1,0:T(8,128)S(1)}, u32[]{:S(2)}, u32[]{:S(2)}) collective-permute-start(f32[8,32,128]{2,1,0:T(8,128)S(1)} %get-tuple-element.19), channel_id=1, source_target_pairs={{0,2},{1,3},{2,0},{3,1},{4,6},{5,7},{6,4},{7,5},{8,10},{9,11},{10,... | collective-permute-start | bytes 393224 | tf_op jit(solution)/shard_map/ppermute | solution.py:180
  9.9 9.2 %collective-permute-start.2 = (f32[8,32,128]{2,1,0:T(8,128)S(1)}, f32[8,32,128]{2,1,0:T(8,128)S(1)}, u32[]{:S(2)}, u32[]{:S(2)}) collective-permute-start(f32[8,32,128]{2,1,0:T(8,128)S(1)} %get-tuple-element.20), channel_id=1, source_target_pairs={{0,3},{1,2},{2,1},{3,0},{4,7},{5,6},{6,5},{7,4},{8,11},{9,10},{10,... | collective-permute-start | bytes 393224 | tf_op jit(solution)/shard_map/ppermute | solution.py:180
  13.4 8.3 %collective-permute-start.12 = (f32[8,32,128]{2,1,0:T(8,128)S(1)}, f32[8,32,128]{2,1,0:T(8,128)S(1)}, u32[]{:S(2)}, u32[]{:S(2)}) collective-permute-start(f32[8,32,128]{2,1,0:T(8,128)S(1)} %add_add_fusion), channel_id=1, source_target_pairs={{0,4},{1,5},{2,6},{3,7},{4,0},{5,1},{6,2},{7,3},{8,12},{9,13},{10,... | collective-permute-start | bytes 393224 | tf_op jit(solution)/shard_map/ppermute | solution.py:180
  19.2 9.2 %collective-permute-start.3 = (f32[8,32,128]{2,1,0:T(8,128)S(1)}, f32[8,32,128]{2,1,0:T(8,128)S(1)}, u32[]{:S(2)}, u32[]{:S(2)}) collective-permute-start(f32[8,32,128]{2,1,0:T(8,128)S(1)} %add_add_fusion.1), channel_id=1, source_target_pairs={{0,4},{1,5},{2,6},{3,7},{4,0},{5,1},{6,2},{7,3},{8,12},{9,13},{10,... | collective-permute-start | bytes 393224 | tf_op jit(solution)/shard_map/ppermute | solution.py:180
  21.7 6.7 %collective-permute-start.13 = (f32[8,32,128]{2,1,0:T(8,128)S(1)}, f32[8,32,128]{2,1,0:T(8,128)S(1)}, u32[]{:S(2)}, u32[]{:S(2)}) collective-permute-start(f32[8,32,128]{2,1,0:T(8,128)S(1)} %add.145), channel_id=1, source_target_pairs={{0,8},{1,9},{2,10},{3,11},{4,12},{5,13},{6,14},{7,15},{8,0},{9,1},... | collective-permute-start | bytes 393224 | tf_op jit(solution)/shard_map/ppermute | solution.py:180
  28.3 1.7 %collective-permute-start.4 = (f32[8,32,128]{2,1,0:T(8,128)S(1)}, f32[8,32,128]{2,1,0:T(8,128)S(1)}, u32[]{:S(2)}, u32[]{:S(2)}) collective-permute-start(f32[8,32,128]{2,1,0:T(8,128)S(1)} %add.126), channel_id=1, source_target_pairs={{0,8},{1,9},{2,10},{3,11},{4,12},{5,13},{6,14},{7,15},{8,0},{9,1},... | collective-permute-start | bytes 393224 | tf_op jit(solution)/shard_map/ppermute | solution.py:180
  28.5 6.4 %collective-permute-start.14 = (f32[8,32,128]{2,1,0:T(8,128)S(1)}, f32[8,32,128]{2,1,0:T(8,128)S(1)}, u32[]{:S(2)}, u32[]{:S(2)}) collective-permute-start(f32[8,32,128]{2,1,0:T(8,128)S(1)} %add.147), channel_id=1, source_target_pairs={{0,16},{1,17},{2,18},{3,19},{4,20},{5,21},{6,22},{7,23},{8,24},{9,... | collective-permute-start | bytes 393224 | tf_op jit(solution)/shard_map/ppermute | solution.py:180
  30.1 8.5 %collective-permute-start.5 = (f32[8,32,128]{2,1,0:T(8,128)S(1)}, f32[8,32,128]{2,1,0:T(8,128)S(1)}, u32[]{:S(2)}, u32[]{:S(2)}) collective-permute-start(f32[8,32,128]{2,1,0:T(8,128)S(1)} %add.128), channel_id=1, source_target_pairs={{0,16},{1,17},{2,18},{3,19},{4,20},{5,21},{6,22},{7,23},{8,24},{9,... | collective-permute-start | bytes 393224 | tf_op jit(solution)/shard_map/ppermute | solution.py:180
  35.1 6.4 %collective-permute-start.16 = (f32[8,32,128]{2,1,0:T(8,128)S(1)}, f32[8,32,128]{2,1,0:T(8,128)S(1)}, u32[]{:S(2)}, u32[]{:S(2)}) collective-permute-start(f32[8,32,128]{2,1,0:T(8,128)S(1)} %get-tuple-element.29), channel_id=1, source_target_pairs={{0,2},{1,3},{2,0},{3,1},{4,6},{5,7},{6,4},{7,5},{8,10},{9,11},{10,... | collective-permute-start | bytes 393224 | tf_op jit(solution)/shard_map/ppermute | solution.py:180
  35.1 8.1 %collective-permute-start.15 = (f32[8,32,128]{2,1,0:T(8,128)S(1)}, f32[8,32,128]{2,1,0:T(8,128)S(1)}, u32[]{:S(2)}, u32[]{:S(2)}) collective-permute-start(f32[8,32,128]{2,1,0:T(8,128)S(1)} %get-tuple-element.30), channel_id=1, source_target_pairs={{0,1},{1,0},{2,3},{3,2},{4,5},{5,4},{6,7},{7,6},{8,9},{9,8},{10,11... | collective-permute-start | bytes 393224 | tf_op jit(solution)/shard_map/ppermute | solution.py:180
  36.2 8.6 %collective-permute-start.17 = (f32[8,32,128]{2,1,0:T(8,128)S(1)}, f32[8,32,128]{2,1,0:T(8,128)S(1)}, u32[]{:S(2)}, u32[]{:S(2)}) collective-permute-start(f32[8,32,128]{2,1,0:T(8,128)S(1)} %get-tuple-element.25), channel_id=1, source_target_pairs={{0,3},{1,2},{2,1},{3,0},{4,7},{5,6},{6,5},{7,4},{8,11},{9,10},{10,... | collective-permute-start | bytes 393224 | tf_op jit(solution)/shard_map/ppermute | solution.py:180
  38.7 3.7 %copy-start.2 = (bf16[128,2048]{1,0:T(8,128)(2,1)S(1)}, bf16[128,2048]{1,0:T(8,128)(2,1)}, u32[]{:S(2)}) copy-start(bf16[128,2048]{1,0:T(8,128)(2,1)} %q_ref.1) | copy-start | bytes 1572868
  38.8 7.9 %collective-permute-start.7 = (f32[8,32,128]{2,1,0:T(8,128)S(1)}, f32[8,32,128]{2,1,0:T(8,128)S(1)}, u32[]{:S(2)}, u32[]{:S(2)}) collective-permute-start(f32[8,32,128]{2,1,0:T(8,128)S(1)} %get-tuple-element.32), channel_id=1, source_target_pairs={{0,2},{1,3},{2,0},{3,1},{4,6},{5,7},{6,4},{7,5},{8,10},{9,11},{10,... | collective-permute-start | bytes 393224 | tf_op jit(solution)/shard_map/ppermute | solution.py:180
  38.9 8.2 %collective-permute-start.6 = (f32[8,32,128]{2,1,0:T(8,128)S(1)}, f32[8,32,128]{2,1,0:T(8,128)S(1)}, u32[]{:S(2)}, u32[]{:S(2)}) collective-permute-start(f32[8,32,128]{2,1,0:T(8,128)S(1)} %get-tuple-element.33), channel_id=1, source_target_pairs={{0,1},{1,0},{2,3},{3,2},{4,5},{5,4},{6,7},{7,6},{8,9},{9,8},{10,11... | collective-permute-start | bytes 393224 | tf_op jit(solution)/shard_map/ppermute | solution.py:180
  41.5 7.1 %collective-permute-start.8 = (f32[8,32,128]{2,1,0:T(8,128)S(1)}, f32[8,32,128]{2,1,0:T(8,128)S(1)}, u32[]{:S(2)}, u32[]{:S(2)}) collective-permute-start(f32[8,32,128]{2,1,0:T(8,128)S(1)} %get-tuple-element.27), channel_id=1, source_target_pairs={{0,3},{1,2},{2,1},{3,0},{4,7},{5,6},{6,5},{7,4},{8,11},{9,10},{10,... | collective-permute-start | bytes 393224 | tf_op jit(solution)/shard_map/ppermute | solution.py:180
  42.4 2.5 %copy-start.3 = (f32[2048]{0:T(1024)S(1)}, f32[2048]{0:T(1024)}, u32[]{:S(2)}) copy-start(f32[2048]{0:T(1024)} %param.7) | copy-start | bytes 24580
where the time goes:
time: 49.8 us; the launch traced here: 49.7 us
  starting transfers between devices  23 us (46%)
  waiting for transfers between devices  21.2 us (43%)
  Pallas kernels  4.8 us (10%)
    ppermute x18, starting transfers between devices, flip(): return lax.ppermute(value, AXES, [(d, d ^ mask) for d in range(size)])  23 us
    ppermute x18, waiting for transfers between devices, flip(): return lax.ppermute(value, AXES, [(d, d ^ mask) for d in range(size)])  21.2 us
    pallas_call x2, Pallas kernels, finish(): pl.pallas_call(functools.partial(finish_body, heads, base), in_specs=[spe...  2.19 us
    pallas_call x1, Pallas kernels, first_states(): pl.pallas_call(functools.partial(first_body, heads), grid_spec=pltpu.Pref...  1.43 us
  transfers between devices with their start and end apart: 18, of which 10 were waited for; matrix products, arithmetic and copies ran while one was open for 1% of the time, Pallas kernels for 5%

commit v1 on v0

--- a/solution.py
+++ b/solution.py
@@ -168,7 +168,7 @@
 ORDER = (1, 3, 2)
 
 
-def on_device(size, queries, keys, values, gain):
+def on_device(size, inner, queries, keys, values, gain):
     _, width = queries.shape
     rank = lax.axis_index(AXES)
     low = rank % WAYS
@@ -196,10 +196,17 @@
             pieces[r] = flip(own[r], r)
         total = functools.reduce(jnp.add, [pieces[r] for r in range(WAYS)])
         before = jnp.zeros_like(total)
-        for b in bits:
+        for b in [b for b in bits if b < inner]:
             other = flip(total, b)
             before = before + jnp.where(rank & b != 0, other, 0.0)
             total = total + other
+        group, earlier = total, jnp.zeros_like(total)
+        for b in [b for b in bits if b > inner]:
+            other = flip(total, b)
+            earlier = earlier + jnp.where(rank & b != 0, other, 0.0)
+            total = total + other
+        other = flip(earlier + jnp.where(rank & inner != 0, 0.0, group), inner)
+        before = before + earlier + other
         carried = []
         for s in range(WAYS):
             part = before
@@ -218,10 +225,11 @@
 
 
 def solution(mesh):
-    size = mesh.shape["outer"] * mesh.shape["inner"]
+    inner = mesh.shape["inner"]
+    size = mesh.shape["outer"] * inner
 
     def body(*args):
-        return on_device(size, *args)
+        return on_device(size, inner, *args)
 
     return jax.shard_map(
         body,

time: 49.8 us -> 49.8 us (level)
  no operation moved by 1% of the time
where the time goes in v1:
time: 49.8 us; the launch traced here: 49.7 us
  starting transfers between devices  22.9 us (46%)
  waiting for transfers between devices  21.4 us (43%)
  Pallas kernels  4.8 us (10%)
    ppermute x18, starting transfers between devices, flip(): return lax.ppermute(value, AXES, [(d, d ^ mask) for d in range(size)])  22.9 us
    ppermute x18, waiting for transfers between devices, flip(): return lax.ppermute(value, AXES, [(d, d ^ mask) for d in range(size)])  21.4 us
    pallas_call x2, Pallas kernels, finish(): pl.pallas_call(functools.partial(finish_body, heads, base), in_specs=[spe...  2.19 us
    pallas_call x1, Pallas kernels, first_states(): pl.pallas_call(functools.partial(first_body, heads), grid_spec=pltpu.Pref...  1.43 us
  transfers between devices with their start and end apart: 18, of which 10 were waited for; matrix products, arithmetic and copies ran while one was open for 1% of the time, Pallas kernels for 5%

profile of v1, /device:TPU:0, one launch (start us, length us, event | category | flops | bytes accessed | tf_op | source)
XLA Modules:
  0.0 49.7 jit_solution(2014656728800021290)
XLA Ops:
  0.0 1.4 %first_states.1 = (f32[8,32,128]{2,1,0:T(8,128)S(1)}, f32[8,32,128]{2,1,0:T(8,128)S(1)}, f32[8,32,128]{2,1,0:T(8,128)S(1)}, f32[8,32,128]{2,1,0:T(8,128)S(1)}) custom-call(s32[1]{0:T(128)} %bitcast.low_ref, bf16[128,2048]{1,0:T(8,128)(2,1)} %k_hbm.1, bf16[128,2048]{1,0:T(8,128)(2,1)} %v_hbm.1), custom_call_target="tpu_custom_call" | custom-call | flops 33554432 | bytes 1048576 | tf_op jit(solution)/shard_map/first_states/pallas_call | solution.py:51
  1.4 3.0 %collective-permute-start.9 = (f32[8,32,128]{2,1,0:T(8,128)S(1)}, f32[8,32,128]{2,1,0:T(8,128)S(1)}, u32[]{:S(2)}, u32[]{:S(2)}) collective-permute-start(f32[8,32,128]{2,1,0:T(8,128)S(1)} %get-tuple-element.22), channel_id=1, source_target_pairs={{0,1},{1,0},{2,3},{3,2},{4,5},{5,4},{6,7},{7,6},{8,9},{9,8},{10,11... | collective-permute-start | bytes 393224 | tf_op jit(solution)/shard_map/ppermute | solution.py:180
  4.5 1.6 %collective-permute-start.10 = (f32[8,32,128]{2,1,0:T(8,128)S(1)}, f32[8,32,128]{2,1,0:T(8,128)S(1)}, u32[]{:S(2)}, u32[]{:S(2)}) collective-permute-start(f32[8,32,128]{2,1,0:T(8,128)S(1)} %get-tuple-element.23), channel_id=1, source_target_pairs={{0,2},{1,3},{2,0},{3,1},{4,6},{5,7},{6,4},{7,5},{8,10},{9,11},{10,... | collective-permute-start | bytes 393224 | tf_op jit(solution)/shard_map/ppermute | solution.py:180
  6.1 0.3 block_states.1
  6.4 2.0 %collective-permute-start = (f32[8,32,128]{2,1,0:T(8,128)S(1)}, f32[8,32,128]{2,1,0:T(8,128)S(1)}, u32[]{:S(2)}, u32[]{:S(2)}) collective-permute-start(f32[8,32,128]{2,1,0:T(8,128)S(1)} %get-tuple-element.18), channel_id=1, source_target_pairs={{0,1},{1,0},{2,3},{3,2},{4,5},{5,4},{6,7},{7,6},{8,9},{9,8},{10,11... | collective-permute-start | bytes 393224 | tf_op jit(solution)/shard_map/ppermute | solution.py:180
  8.3 1.6 %collective-permute-start.1 = (f32[8,32,128]{2,1,0:T(8,128)S(1)}, f32[8,32,128]{2,1,0:T(8,128)S(1)}, u32[]{:S(2)}, u32[]{:S(2)}) collective-permute-start(f32[8,32,128]{2,1,0:T(8,128)S(1)} %get-tuple-element.19), channel_id=1, source_target_pairs={{0,2},{1,3},{2,0},{3,1},{4,6},{5,7},{6,4},{7,5},{8,10},{9,11},{10,... | collective-permute-start | bytes 393224 | tf_op jit(solution)/shard_map/ppermute | solution.py:180
  9.9 1.0 %collective-permute-start.2 = (f32[8,32,128]{2,1,0:T(8,128)S(1)}, f32[8,32,128]{2,1,0:T(8,128)S(1)}, u32[]{:S(2)}, u32[]{:S(2)}) collective-permute-start(f32[8,32,128]{2,1,0:T(8,128)S(1)} %get-tuple-element.20), channel_id=1, source_target_pairs={{0,3},{1,2},{2,1},{3,0},{4,7},{5,6},{6,5},{7,4},{8,11},{9,10},{10,... | collective-permute-start | bytes 393224 | tf_op jit(solution)/shard_map/ppermute | solution.py:180
  11.0 2.4 %collective-permute-done.11 = f32[8,32,128]{2,1,0:T(8,128)S(1)} collective-permute-done((f32[8,32,128]{2,1,0:T(8,128)S(1)}, f32[8,32,128]{2,1,0:T(8,128)S(1)}, u32[]{:S(2)}, u32[]{:S(2)}) %collective-permute-start.11) | collective-permute-done | bytes 131104 | tf_op jit(solution)/shard_map/ppermute | solution.py:180
  13.4 2.7 %collective-permute-start.12 = (f32[8,32,128]{2,1,0:T(8,128)S(1)}, f32[8,32,128]{2,1,0:T(8,128)S(1)}, u32[]{:S(2)}, u32[]{:S(2)}) collective-permute-start(f32[8,32,128]{2,1,0:T(8,128)S(1)} %add_add_fusion.1), channel_id=1, source_target_pairs={{0,4},{1,5},{2,6},{3,7},{4,0},{5,1},{6,2},{7,3},{8,12},{9,13},{10,... | collective-permute-start | bytes 393224 | tf_op jit(solution)/shard_map/ppermute | solution.py:180
  16.1 1.8 %collective-permute-done.1 = f32[8,32,128]{2,1,0:T(8,128)S(1)} collective-permute-done((f32[8,32,128]{2,1,0:T(8,128)S(1)}, f32[8,32,128]{2,1,0:T(8,128)S(1)}, u32[]{:S(2)}, u32[]{:S(2)}) %collective-permute-start.1) | collective-permute-done | bytes 131104 | tf_op jit(solution)/shard_map/ppermute | solution.py:180
  17.9 1.3 %collective-permute-done.2 = f32[8,32,128]{2,1,0:T(8,128)S(1)} collective-permute-done((f32[8,32,128]{2,1,0:T(8,128)S(1)}, f32[8,32,128]{2,1,0:T(8,128)S(1)}, u32[]{:S(2)}, u32[]{:S(2)}) %collective-permute-start.2) | collective-permute-done | bytes 131104 | tf_op jit(solution)/shard_map/ppermute | solution.py:180
  19.2 2.5 %collective-permute-start.3 = (f32[8,32,128]{2,1,0:T(8,128)S(1)}, f32[8,32,128]{2,1,0:T(8,128)S(1)}, u32[]{:S(2)}, u32[]{:S(2)}) collective-permute-start(f32[8,32,128]{2,1,0:T(8,128)S(1)} %add_add_fusion.3), channel_id=1, source_target_pairs={{0,4},{1,5},{2,6},{3,7},{4,0},{5,1},{6,2},{7,3},{8,12},{9,13},{10,... | collective-permute-start | bytes 393224 | tf_op jit(solution)/shard_map/ppermute | solution.py:180
  21.7 1.6 %collective-permute-start.13 = (f32[8,32,128]{2,1,0:T(8,128)S(1)}, f32[8,32,128]{2,1,0:T(8,128)S(1)}, u32[]{:S(2)}, u32[]{:S(2)}) collective-permute-start(f32[8,32,128]{2,1,0:T(8,128)S(1)} %add.145), channel_id=1, source_target_pairs={{0,16},{1,17},{2,18},{3,19},{4,20},{5,21},{6,22},{7,23},{8,24},{9,... | collective-permute-start | bytes 393224 | tf_op jit(solution)/shard_map/ppermute | solution.py:180
  23.3 5.0 %collective-permute-done.3 = f32[8,32,128]{2,1,0:T(8,128)S(1)} collective-permute-done((f32[8,32,128]{2,1,0:T(8,128)S(1)}, f32[8,32,128]{2,1,0:T(8,128)S(1)}, u32[]{:S(2)}, u32[]{:S(2)}) %collective-permute-start.3) | collective-permute-done | bytes 131104 | tf_op jit(solution)/shard_map/ppermute | solution.py:180
  28.3 1.6 %collective-permute-start.4 = (f32[8,32,128]{2,1,0:T(8,128)S(1)}, f32[8,32,128]{2,1,0:T(8,128)S(1)}, u32[]{:S(2)}, u32[]{:S(2)}) collective-permute-start(f32[8,32,128]{2,1,0:T(8,128)S(1)} %add.126), channel_id=1, source_target_pairs={{0,16},{1,17},{2,18},{3,19},{4,20},{5,21},{6,22},{7,23},{8,24},{9,... | collective-permute-start | bytes 393224 | tf_op jit(solution)/shard_map/ppermute | solution.py:180
  30.0 3.8 %collective-permute-done.4 = f32[8,32,128]{2,1,0:T(8,128)S(1)} collective-permute-done((f32[8,32,128]{2,1,0:T(8,128)S(1)}, f32[8,32,128]{2,1,0:T(8,128)S(1)}, u32[]{:S(2)}, u32[]{:S(2)}) %collective-permute-start.4) | collective-permute-done | bytes 131104 | tf_op jit(solution)/shard_map/ppermute | solution.py:180
  34.0 0.1 select_add_fusion.1
  34.2 0.7 %collective-permute-start.15 = (f32[8,32,128]{2,1,0:T(8,128)S(1)}, f32[8,32,128]{2,1,0:T(8,128)S(1)}, u32[]{:S(2)}, u32[]{:S(2)}) collective-permute-start(f32[8,32,128]{2,1,0:T(8,128)S(1)} %get-tuple-element.30), channel_id=1, source_target_pairs={{0,1},{1,0},{2,3},{3,2},{4,5},{5,4},{6,7},{7,6},{8,9},{9,8},{10,11... | collective-permute-start | bytes 393224 | tf_op jit(solution)/shard_map/ppermute | solution.py:180
  34.8 2.8 %collective-permute-start.17 = (f32[8,32,128]{2,1,0:T(8,128)S(1)}, f32[8,32,128]{2,1,0:T(8,128)S(1)}, u32[]{:S(2)}, u32[]{:S(2)}) collective-permute-start(f32[8,32,128]{2,1,0:T(8,128)S(1)} %get-tuple-element.25), channel_id=1, source_target_pairs={{0,3},{1,2},{2,1},{3,0},{4,7},{5,6},{6,5},{7,4},{8,11},{9,10},{10,... | collective-permute-start | bytes 393224 | tf_op jit(solution)/shard_map/ppermute | solution.py:180
  37.7 0.1 select_add_fusion.5
  37.8 0.1 select_add_fusion.6
  37.9 0.1 collective-permute-start.7
  38.0 0.6 %collective-permute-start.6 = (f32[8,32,128]{2,1,0:T(8,128)S(1)}, f32[8,32,128]{2,1,0:T(8,128)S(1)}, u32[]{:S(2)}, u32[]{:S(2)}) collective-permute-start(f32[8,32,128]{2,1,0:T(8,128)S(1)} %get-tuple-element.33), channel_id=1, source_target_pairs={{0,1},{1,0},{2,3},{3,2},{4,5},{5,4},{6,7},{7,6},{8,9},{9,8},{10,11... | collective-permute-start | bytes 393224 | tf_op jit(solution)/shard_map/ppermute | solution.py:180
  38.6 2.0 %collective-permute-done.16.refs_2_ = f32[8,32,128]{2,1,0:T(8,128)S(1)} collective-permute-done((f32[8,32,128]{2,1,0:T(8,128)S(1)}, f32[8,32,128]{2,1,0:T(8,128)S(1)}, u32[]{:S(2)}, u32[]{:S(2)}) %collective-permute-start.16) | collective-permute-done | bytes 131104 | tf_op jit(solution)/shard_map/ppermute | solution.py:180
  40.5 0.9 %collective-permute-start.8 = (f32[8,32,128]{2,1,0:T(8,128)S(1)}, f32[8,32,128]{2,1,0:T(8,128)S(1)}, u32[]{:S(2)}, u32[]{:S(2)}) collective-permute-start(f32[8,32,128]{2,1,0:T(8,128)S(1)} %get-tuple-element.27), channel_id=1, source_target_pairs={{0,3},{1,2},{2,1},{3,0},{4,7},{5,6},{6,5},{7,4},{8,11},{9,10},{10,... | collective-permute-start | bytes 393224 | tf_op jit(solution)/shard_map/ppermute | solution.py:180
  41.4 0.9 %within_block.1 = (f32[128,2048]{1,0:T(8,128)S(1)}, bf16[128,2048]{1,0:T(8,128)(2,1)S(1)}) custom-call(s32[1]{0:T(128)} %bitcast.low_ref, bf16[128,2048]{1,0:T(8,128)(2,1)S(1)} %copy-done.2, bf16[128,2048]{1,0:T(8,128)(2,1)S(1)} %copy-done, bf16[128,2048]{1,0:T(8,128)(2,1)S(1)} %copy-done.1), custom_call_target="tpu_custom_call" | custom-call | flops 201326592 | bytes 3145728 | tf_op jit(solution)/shard_map/within_block/pallas_call | solution.py:124
  42.3 0.6 %collective-permute-done.15.refs_1_ = f32[8,32,128]{2,1,0:T(8,128)S(1)} collective-permute-done((f32[8,32,128]{2,1,0:T(8,128)S(1)}, f32[8,32,128]{2,1,0:T(8,128)S(1)}, u32[]{:S(2)}, u32[]{:S(2)}) %collective-permute-start.15) | collective-permute-done | bytes 131104 | tf_op jit(solution)/shard_map/ppermute | solution.py:180
  42.9 0.5 %collective-permute-done.17.refs_3_ = f32[8,32,128]{2,1,0:T(8,128)S(1)} collective-permute-done((f32[8,32,128]{2,1,0:T(8,128)S(1)}, f32[8,32,128]{2,1,0:T(8,128)S(1)}, u32[]{:S(2)}, u32[]{:S(2)}) %collective-permute-start.17) | collective-permute-done | bytes 131104 | tf_op jit(solution)/shard_map/ppermute | solution.py:180
  43.4 1.1 %finish.2.refs_4_ = bf16[128,2048]{1,0:T(8,128)(2,1)} custom-call(bf16[128,2048]{1,0:T(8,128)(2,1)S(1)} %get-tuple-element.15.q_ref, f32[128,2048]{1,0:T(8,128)S(1)} %get-tuple-element.16.near_ref, f32[1,2048]{1,0:T(1,128)S(1)} %bitcast.2, f32[8,32,128]{2,1,0:T(8,128)S(1)} %get-tuple-element.31.refs_0_, f32[8,32,128]{2,1,0:T(8,128)S(1)} %collective-permute-done.15.refs_1_, ...), custom_call_target="tpu_custom_call" | custom-call | flops 33554432 | bytes 1572864 | tf_op jit(solution)/shard_map/finish/pallas_call | solution.py:153
  44.5 1.7 %collective-permute-done.7.refs_2_ = f32[8,32,128]{2,1,0:T(8,128)S(1)} collective-permute-done((f32[8,32,128]{2,1,0:T(8,128)S(1)}, f32[8,32,128]{2,1,0:T(8,128)S(1)}, u32[]{:S(2)}, u32[]{:S(2)}) %collective-permute-start.7) | collective-permute-done | bytes 131104 | tf_op jit(solution)/shard_map/ppermute | solution.py:180
  46.2 2.3 %collective-permute-done.8.refs_3_ = f32[8,32,128]{2,1,0:T(8,128)S(1)} collective-permute-done((f32[8,32,128]{2,1,0:T(8,128)S(1)}, f32[8,32,128]{2,1,0:T(8,128)S(1)}, u32[]{:S(2)}, u32[]{:S(2)}) %collective-permute-start.8) | collective-permute-done | bytes 131104 | tf_op jit(solution)/shard_map/ppermute | solution.py:180
  48.6 1.1 %finish.3 = bf16[128,2048]{1,0:T(8,128)(2,1)} custom-call(bf16[128,2048]{1,0:T(8,128)(2,1)S(1)} %get-tuple-element.15.q_ref, f32[128,2048]{1,0:T(8,128)S(1)} %get-tuple-element.16.near_ref, f32[1,2048]{1,0:T(1,128)S(1)} %bitcast.3, f32[8,32,128]{2,1,0:T(8,128)S(1)} %get-tuple-element.34.refs_0_, ...), custom_call_target="tpu_custom_call", output_to_operand_aliasing={{}: (7, {})} | custom-call | flops 33554432 | bytes 1572864 | tf_op jit(solution)/shard_map/finish/pallas_call | solution.py:153
  (27 shorter events, 0.5 us)
Async XLA Ops:
  0.0 6.1 %copy-start = (bf16[128,2048]{1,0:T(8,128)(2,1)S(1)}, bf16[128,2048]{1,0:T(8,128)(2,1)}, u32[]{:S(2)}) copy-start(bf16[128,2048]{1,0:T(8,128)(2,1)} %k_hbm.1) | copy-start | bytes 1572868
  0.0 6.1 %copy-start.1 = (bf16[128,2048]{1,0:T(8,128)(2,1)S(1)}, bf16[128,2048]{1,0:T(8,128)(2,1)}, u32[]{:S(2)}) copy-start(bf16[128,2048]{1,0:T(8,128)(2,1)} %v_hbm.1) | copy-start | bytes 1572868
  1.4 8.5 %collective-permute-start.9 = (f32[8,32,128]{2,1,0:T(8,128)S(1)}, f32[8,32,128]{2,1,0:T(8,128)S(1)}, u32[]{:S(2)}, u32[]{:S(2)}) collective-permute-start(f32[8,32,128]{2,1,0:T(8,128)S(1)} %get-tuple-element.22), channel_id=1, source_target_pairs={{0,1},{1,0},{2,3},{3,2},{4,5},{5,4},{6,7},{7,6},{8,9},{9,8},{10,11... | collective-permute-start | bytes 393224 | tf_op jit(solution)/shard_map/ppermute | solution.py:180
  4.5 6.5 %collective-permute-start.10 = (f32[8,32,128]{2,1,0:T(8,128)S(1)}, f32[8,32,128]{2,1,0:T(8,128)S(1)}, u32[]{:S(2)}, u32[]{:S(2)}) collective-permute-start(f32[8,32,128]{2,1,0:T(8,128)S(1)} %get-tuple-element.23), channel_id=1, source_target_pairs={{0,2},{1,3},{2,0},{3,1},{4,6},{5,7},{6,4},{7,5},{8,10},{9,11},{10,... | collective-permute-start | bytes 393224 | tf_op jit(solution)/shard_map/ppermute | solution.py:180
  6.1 7.3 %collective-permute-start.11 = (f32[8,32,128]{2,1,0:T(8,128)S(1)}, f32[8,32,128]{2,1,0:T(8,128)S(1)}, u32[]{:S(2)}, u32[]{:S(2)}) collective-permute-start(f32[8,32,128]{2,1,0:T(8,128)S(1)} %get-tuple-element.24), channel_id=1, source_target_pairs={{0,3},{1,2},{2,1},{3,0},{4,7},{5,6},{6,5},{7,4},{8,11},{9,10},{10,... | collective-permute-start | bytes 393224 | tf_op jit(solution)/shard_map/ppermute | solution.py:180
  6.4 9.7 %collective-permute-start = (f32[8,32,128]{2,1,0:T(8,128)S(1)}, f32[8,32,128]{2,1,0:T(8,128)S(1)}, u32[]{:S(2)}, u32[]{:S(2)}) collective-permute-start(f32[8,32,128]{2,1,0:T(8,128)S(1)} %get-tuple-element.18), channel_id=1, source_target_pairs={{0,1},{1,0},{2,3},{3,2},{4,5},{5,4},{6,7},{7,6},{8,9},{9,8},{10,11... | collective-permute-start | bytes 393224 | tf_op jit(solution)/shard_map/ppermute | solution.py:180
  8.3 9.5 %collective-permute-start.1 = (f32[8,32,128]{2,1,0:T(8,128)S(1)}, f32[8,32,128]{2,1,0:T(8,128)S(1)}, u32[]{:S(2)}, u32[]{:S(2)}) collective-permute-start(f32[8,32,128]{2,1,0:T(8,128)S(1)} %get-tuple-element.19), channel_id=1, source_target_pairs={{0,2},{1,3},{2,0},{3,1},{4,6},{5,7},{6,4},{7,5},{8,10},{9,11},{10,... | collective-permute-start | bytes 393224 | tf_op jit(solution)/shard_map/ppermute | solution.py:180
  9.9 9.2 %collective-permute-start.2 = (f32[8,32,128]{2,1,0:T(8,128)S(1)}, f32[8,32,128]{2,1,0:T(8,128)S(1)}, u32[]{:S(2)}, u32[]{:S(2)}) collective-permute-start(f32[8,32,128]{2,1,0:T(8,128)S(1)} %get-tuple-element.20), channel_id=1, source_target_pairs={{0,3},{1,2},{2,1},{3,0},{4,7},{5,6},{6,5},{7,4},{8,11},{9,10},{10,... | collective-permute-start | bytes 393224 | tf_op jit(solution)/shard_map/ppermute | solution.py:180
  13.4 8.3 %collective-permute-start.12 = (f32[8,32,128]{2,1,0:T(8,128)S(1)}, f32[8,32,128]{2,1,0:T(8,128)S(1)}, u32[]{:S(2)}, u32[]{:S(2)}) collective-permute-start(f32[8,32,128]{2,1,0:T(8,128)S(1)} %add_add_fusion.1), channel_id=1, source_target_pairs={{0,4},{1,5},{2,6},{3,7},{4,0},{5,1},{6,2},{7,3},{8,12},{9,13},{10,... | collective-permute-start | bytes 393224 | tf_op jit(solution)/shard_map/ppermute | solution.py:180
  19.2 9.2 %collective-permute-start.3 = (f32[8,32,128]{2,1,0:T(8,128)S(1)}, f32[8,32,128]{2,1,0:T(8,128)S(1)}, u32[]{:S(2)}, u32[]{:S(2)}) collective-permute-start(f32[8,32,128]{2,1,0:T(8,128)S(1)} %add_add_fusion.3), channel_id=1, source_target_pairs={{0,4},{1,5},{2,6},{3,7},{4,0},{5,1},{6,2},{7,3},{8,12},{9,13},{10,... | collective-permute-start | bytes 393224 | tf_op jit(solution)/shard_map/ppermute | solution.py:180
  21.7 8.2 %collective-permute-start.13 = (f32[8,32,128]{2,1,0:T(8,128)S(1)}, f32[8,32,128]{2,1,0:T(8,128)S(1)}, u32[]{:S(2)}, u32[]{:S(2)}) collective-permute-start(f32[8,32,128]{2,1,0:T(8,128)S(1)} %add.145), channel_id=1, source_target_pairs={{0,16},{1,17},{2,18},{3,19},{4,20},{5,21},{6,22},{7,23},{8,24},{9,... | collective-permute-start | bytes 393224 | tf_op jit(solution)/shard_map/ppermute | solution.py:180
  28.3 5.5 %collective-permute-start.4 = (f32[8,32,128]{2,1,0:T(8,128)S(1)}, f32[8,32,128]{2,1,0:T(8,128)S(1)}, u32[]{:S(2)}, u32[]{:S(2)}) collective-permute-start(f32[8,32,128]{2,1,0:T(8,128)S(1)} %add.126), channel_id=1, source_target_pairs={{0,16},{1,17},{2,18},{3,19},{4,20},{5,21},{6,22},{7,23},{8,24},{9,... | collective-permute-start | bytes 393224 | tf_op jit(solution)/shard_map/ppermute | solution.py:180
  29.9 4.0 %collective-permute-start.14 = (f32[8,32,128]{2,1,0:T(8,128)S(1)}, f32[8,32,128]{2,1,0:T(8,128)S(1)}, u32[]{:S(2)}, u32[]{:S(2)}) collective-permute-start(f32[8,32,128]{2,1,0:T(8,128)S(1)} %select_add_fusion.4), channel_id=1, source_target_pairs={{0,8},{1,9},{2,10},{3,11},{4,12},{5,13},{6,14},{7,15},{8,0},{9,1},... | collective-permute-start | bytes 393224 | tf_op jit(solution)/shard_map/ppermute | solution.py:180
  33.8 3.8 %collective-permute-start.5 = (f32[8,32,128]{2,1,0:T(8,128)S(1)}, f32[8,32,128]{2,1,0:T(8,128)S(1)}, u32[]{:S(2)}, u32[]{:S(2)}) collective-permute-start(f32[8,32,128]{2,1,0:T(8,128)S(1)} %select_add_fusion.9), channel_id=1, source_target_pairs={{0,8},{1,9},{2,10},{3,11},{4,12},{5,13},{6,14},{7,15},{8,0},{9,1},... | collective-permute-start | bytes 393224 | tf_op jit(solution)/shard_map/ppermute | solution.py:180
  34.1 6.4 %collective-permute-start.16 = (f32[8,32,128]{2,1,0:T(8,128)S(1)}, f32[8,32,128]{2,1,0:T(8,128)S(1)}, u32[]{:S(2)}, u32[]{:S(2)}) collective-permute-start(f32[8,32,128]{2,1,0:T(8,128)S(1)} %get-tuple-element.29), channel_id=1, source_target_pairs={{0,2},{1,3},{2,0},{3,1},{4,6},{5,7},{6,4},{7,5},{8,10},{9,11},{10,... | collective-permute-start | bytes 393224 | tf_op jit(solution)/shard_map/ppermute | solution.py:180
  34.2 8.7 %collective-permute-start.15 = (f32[8,32,128]{2,1,0:T(8,128)S(1)}, f32[8,32,128]{2,1,0:T(8,128)S(1)}, u32[]{:S(2)}, u32[]{:S(2)}) collective-permute-start(f32[8,32,128]{2,1,0:T(8,128)S(1)} %get-tuple-element.30), channel_id=1, source_target_pairs={{0,1},{1,0},{2,3},{3,2},{4,5},{5,4},{6,7},{7,6},{8,9},{9,8},{10,11... | collective-permute-start | bytes 393224 | tf_op jit(solution)/shard_map/ppermute | solution.py:180
  34.8 8.6 %collective-permute-start.17 = (f32[8,32,128]{2,1,0:T(8,128)S(1)}, f32[8,32,128]{2,1,0:T(8,128)S(1)}, u32[]{:S(2)}, u32[]{:S(2)}) collective-permute-start(f32[8,32,128]{2,1,0:T(8,128)S(1)} %get-tuple-element.25), channel_id=1, source_target_pairs={{0,3},{1,2},{2,1},{3,0},{4,7},{5,6},{6,5},{7,4},{8,11},{9,10},{10,... | collective-permute-start | bytes 393224 | tf_op jit(solution)/shard_map/ppermute | solution.py:180
  37.7 3.7 %copy-start.2 = (bf16[128,2048]{1,0:T(8,128)(2,1)S(1)}, bf16[128,2048]{1,0:T(8,128)(2,1)}, u32[]{:S(2)}) copy-start(bf16[128,2048]{1,0:T(8,128)(2,1)} %q_ref.1) | copy-start | bytes 1572868
  37.9 8.4 %collective-permute-start.7 = (f32[8,32,128]{2,1,0:T(8,128)S(1)}, f32[8,32,128]{2,1,0:T(8,128)S(1)}, u32[]{:S(2)}, u32[]{:S(2)}) collective-permute-start(f32[8,32,128]{2,1,0:T(8,128)S(1)} %get-tuple-element.32), channel_id=1, source_target_pairs={{0,2},{1,3},{2,0},{3,1},{4,6},{5,7},{6,4},{7,5},{8,10},{9,11},{10,... | collective-permute-start | bytes 393224 | tf_op jit(solution)/shard_map/ppermute | solution.py:180
  38.0 8.3 %collective-permute-start.6 = (f32[8,32,128]{2,1,0:T(8,128)S(1)}, f32[8,32,128]{2,1,0:T(8,128)S(1)}, u32[]{:S(2)}, u32[]{:S(2)}) collective-permute-start(f32[8,32,128]{2,1,0:T(8,128)S(1)} %get-tuple-element.33), channel_id=1, source_target_pairs={{0,1},{1,0},{2,3},{3,2},{4,5},{5,4},{6,7},{7,6},{8,9},{9,8},{10,11... | collective-permute-start | bytes 393224 | tf_op jit(solution)/shard_map/ppermute | solution.py:180
  40.5 8.0 %collective-permute-start.8 = (f32[8,32,128]{2,1,0:T(8,128)S(1)}, f32[8,32,128]{2,1,0:T(8,128)S(1)}, u32[]{:S(2)}, u32[]{:S(2)}) collective-permute-start(f32[8,32,128]{2,1,0:T(8,128)S(1)} %get-tuple-element.27), channel_id=1, source_target_pairs={{0,3},{1,2},{2,1},{3,0},{4,7},{5,6},{6,5},{7,4},{8,11},{9,10},{10,... | collective-permute-start | bytes 393224 | tf_op jit(solution)/shard_map/ppermute | solution.py:180
  41.4 2.0 %copy-start.3 = (f32[2048]{0:T(1024)S(1)}, f32[2048]{0:T(1024)}, u32[]{:S(2)}) copy-start(f32[2048]{0:T(1024)} %param.7) | copy-start | bytes 24580
